TPU v7x, 32 devices: a whole 2x2x4 slice. The times are simulated.
32 devices in a mesh: groups: 2 (over x), rows: 16 (over z, y, core).
Axes of the slice: x: 2, y: 2, z: 4, core: 2. Of those that a mesh axis runs over, the one named last changes fastest.
Arguments:
- block_input: bfloat16 [512, 352, 512], P(('groups', 'rows')), parts along dimension 0, may hold values from -6 to 6
- first_pre: bfloat16 [512, 352, 128], P(('groups', 'rows')), parts along dimension 0, may hold values from -6 to 6
- second_pre: bfloat16 [512, 352, 128], P(('groups', 'rows')), parts along dimension 0, may hold values from -6 to 6
- output_pre: bfloat16 [512, 352, 512], P(('groups', 'rows')), parts along dimension 0, may hold values from -6 to 6
- output_grad: bfloat16 [512, 352, 512], P('groups', None, 'rows'), parts along dimension 0, may hold values from -6 to 6
- first_weight: bfloat16 [512, 128], replicated, may hold values from -0.25 to 0.25
- middle_weight: bfloat16 [3, 3, 128, 128], replicated, may hold values from -0.1875 to 0.1875
- last_weight: bfloat16 [128, 512], replicated, may hold values from -0.5 to 0.5
Outputs:
- input_grad: bfloat16 [512, 352, 512], P(('groups', 'rows')), parts along dimension 0
- first_weight_grad: float32 [1024, 128], P(('groups', 'rows')), parts along dimension 0
- middle_weight_grad: float32 [6, 3, 128, 128], P('groups'), parts along dimension 0
- last_weight_grad: float32 [256, 512], P('groups'), parts along dimension 0
There are 2 independent parts, one for each index of `groups`. A program takes and returns all parts, laid end to end along the dimension named above; an argument that names none is the same for every part. Nothing has to cross between parts.
All inputs are finite; a program needn't handle non-finite values.
Results may differ from a plain program's by a relative error of at most 0.0049.
Values may be sent and summed in bfloat16 or wider, within the bound.
No kernel may reach another device: no remote copies, remote signals or barrier semaphores. Data moves between devices by JAX's collectives and lax.ppermute only.
A program may use at most 128 MiB of HBM per device.

v0:
```python
import math
import jax
import jax.numpy as jnp
from jax import lax
from jax.sharding import PartitionSpec as P


def with_halo(value, sides, width):
    for axis, dim in sides:
        size, length = (lax.axis_size(axis), value.shape[dim])
        up = [(i, (i + 1) % size) for i in range(size - 1)]
        down = [(j, i) for i, j in up]
        last = lax.slice_in_dim(value, length - width, length, axis=dim)
        leading = lax.slice_in_dim(value, 0, width, axis=dim)
        before = lax.ppermute(last, axis, up)
        after = lax.ppermute(leading, axis, down)
        value = jnp.concatenate([before, value, after], axis=dim)
    return value


def contract_rows(left, right):
    return lax.dot_general(
        left, right, (((0,), (0,)), ((), ())), preferred_element_type=jnp.float32
    )


def shards(
    block_input,
    first_pre,
    second_pre,
    output_pre,
    output_grad,
    first_weight,
    middle_weight,
    last_weight,
):
    tile_rows, map_cols, channels = block_input.shape
    inner_width = first_pre.shape[2]
    pixels = tile_rows * map_cols
    factor = 1.0 / math.sqrt(pixels * lax.axis_size("rows"))
    spatial = lax.all_to_all(output_grad, "rows", split_axis=0, concat_axis=2, tiled=True)
    masked_out = jnp.where(output_pre > 0, spatial, jnp.zeros_like(spatial))
    second_act = jnp.maximum(second_pre, jnp.zeros_like(second_pre))
    first_act = jnp.maximum(first_pre, jnp.zeros_like(first_pre))
    out_flat = masked_out.reshape(pixels, channels)
    last_part = contract_rows(second_act.reshape(pixels, inner_width), out_flat)
    last_total = lax.psum(last_part, "rows")
    inner = lax.dot_general(
        out_flat, last_weight, (((1,), (1,)), ((), ())), preferred_element_type=jnp.float32
    )
    second_grad = jnp.where(second_pre.reshape(pixels, inner_width) > 0, inner, 0.0).astype(
        jnp.bfloat16
    )
    second_flat = second_grad
    second_grad = second_flat.reshape(tile_rows, map_cols, inner_width)
    act_ext = with_halo(first_act, (("rows", 0),), 1)
    act_padded = jnp.pad(act_ext, ((0, 0), (1, 1), (0, 0)))
    taps = []
    for row_tap in range(3):
        line = []
        for col_tap in range(3):
            window = act_padded[
                row_tap : row_tap + tile_rows, col_tap : col_tap + map_cols
            ].reshape(pixels, inner_width)
            line.append(contract_rows(window, second_flat))
        taps.append(jnp.stack(line))
    middle_part = jnp.stack(taps)
    grad_ext = with_halo(second_grad, (("rows", 0),), 1)
    grad_padded = jnp.pad(grad_ext, ((0, 0), (1, 1), (0, 0)))
    total = jnp.zeros((pixels, inner_width), jnp.float32)
    for row_tap in range(3):
        for col_tap in range(3):
            moved = grad_padded[
                2 - row_tap : 2 - row_tap + tile_rows, 2 - col_tap : 2 - col_tap + map_cols
            ].reshape(pixels, inner_width)
            total = total + lax.dot_general(
                moved,
                middle_weight[row_tap, col_tap],
                (((1,), (1,)), ((), ())),
                preferred_element_type=jnp.float32,
            )
    first_grad = jnp.where(first_pre.reshape(pixels, inner_width) > 0, total, 0.0).astype(
        jnp.bfloat16
    )
    input_flat = block_input.reshape(pixels, channels)
    first_wgrad = (
        lax.psum_scatter(
            contract_rows(input_flat, first_grad), "rows", scatter_dimension=0, tiled=True
        )
        * factor
    )
    back = lax.dot_general(
        first_grad, first_weight, (((1,), (1,)), ((), ())), preferred_element_type=jnp.float32
    )
    input_grad = (
        (back + out_flat.astype(jnp.float32))
        .astype(jnp.bfloat16)
        .reshape(tile_rows, map_cols, channels)
    )
    middle_total = lax.psum(middle_part, "rows")
    return (input_grad, first_wgrad, middle_total * factor, last_total * factor)


def solution(mesh):
    placed = (
        P(("groups", "rows"), None, None),
        P(("groups", "rows"), None, None),
        P(("groups", "rows"), None, None),
        P(("groups", "rows"), None, None),
        P("groups", None, "rows"),
        P(),
        P(),
        P(),
    )
    return jax.shard_map(
        shards,
        mesh=mesh,
        in_specs=placed,
        out_specs=(
            P(("groups", "rows"), None, None),
            P(("groups", "rows"), None),
            P("groups", None, None, None),
            P("groups", None),
        ),
        check_vma=False,
    )
```

profile of v0, /device:TPU:0, one launch (start us, length us, event | category | flops | bytes accessed | tf_op | source)
XLA Modules:
  0.0 376.6 jit_solution(985985323894171516)
XLA Ops:
  7.2 9.7 %copy.21 = bf16[256,352,32]{1,2,0:T(8,128)(2,1)} copy(bf16[256,352,32]{0,2,1:T(8,128)(2,1)} %param.12) | data formatting | bytes 11534336 | tf_op args[4]
  16.8 7.6 %all-to-all-start = ((bf16[256,352,32]{1,2,0:T(8,128)(2,1)}), bf16[256,352,32]{1,2,0:T(8,128)(2,1)}, u32[]{:S(2)}, u32[]{:S(2)}) async-start(bf16[256,352,32]{1,2,0:T(8,128)(2,1)} %copy.21), calls=%async_computation | async-start | bytes 12582912 | tf_op jit(solution)/shard_map/all_to_all | solution.py:41
  24.6 2.4 collective-permute-start.2
  27.0 1.3 collective-permute-start.3
  28.3 1.3 broadcast_compare_fusion.1
  29.6 1.3 broadcast_compare_fusion
  30.9 8.3 %copy.20 = bf16[16,352,512]{1,2,0:T(8,128)(2,1)} copy(bf16[16,352,512]{2,1,0:T(8,128)(2,1)} %param.11) | data formatting | bytes 11534336 | tf_op args[3]
  39.2 1.7 pad_maximum_fusion.1
  41.4 3.9 %fusion.33 = (bf16[16,352,128]{2,1,0:T(8,128)(2,1)}, bf16[16,352,128]{2,1,0:T(8,128)(2,1)}, bf16[16,352,128]{2,1,0:T(8,128)(2,1)}, bf16[16,352,128]{2,1,0:T(8,12...) fusion(bf16[18,354,128]{2,1,0:T(8,128)(2,1)S(1)} %select_maximum_fusion), kind=kLoop, calls=%fused_computation.73 | loop fusion | bytes 17301504 | tf_op jit(solution)/shard_map/slice | solution.py:62
  45.3 93.3 %all-to-all-done = bf16[256,352,32]{1,2,0:T(8,128)(2,1)} async-done(((bf16[256,352,32]{1,2,0:T(8,128)(2,1)}), bf16[256,352,32]{1,2,0:T(8,128)(2,1)}, u32[]{:S(2)}, u32[]{:S(2)}) %all-to-all-start) | async-done | bytes 5767200 | tf_op jit(solution)/shard_map/all_to_all | solution.py:41
  138.6 6.4 %copy.22 = bf16[16,352,16,32]{1,3,2,0:T(8,128)(2,1)} copy(bf16[16,352,16,32]{1,3,0,2:T(8,128)(2,1)} %bitcast.3) | data formatting | bytes 11534336 | tf_op jit(solution)/shard_map/all_to_all | solution.py:41
  145.0 8.0 %compare_select_fusion = bf16[16,352,512]{1,2,0:T(8,128)(2,1)} fusion(bf16[16,352,512]{1,2,0:T(8,128)(2,1)} %copy.20, bf16[16,352,16,32]{1,3,2,0:T(8,128)(2,1)} %copy.22), kind=kLoop, calls=%fused_computation | loop fusion | flops 5767168 | bytes 17301504 | tf_op jit(solution)/shard_map/jit(_where)/select_n | solution.py:42
  153.1 8.5 %copy.23 = bf16[16,352,512]{2,1,0:T(8,128)(2,1)} copy(bf16[16,352,512]{1,2,0:T(8,128)(2,1)} %compare_select_fusion) | data formatting | bytes 11534336 | tf_op jit(solution)/shard_map/jit(_where)/select_n | solution.py:42
  161.6 5.8 %fusion.8 = f32[128,512]{1,0:T(8,128)} fusion(bf16[16,352,512]{1,2,0:T(8,128)(2,1)} %compare_select_fusion, bf16[16,352,128]{2,1,0:T(8,128)(2,1)S(1)} %copy-done.12), kind=kOutput, calls=%fused_computation.28 | convolution fusion | flops 738918400 | bytes 7471104 | tf_op jit(solution)/shard_map/dot_general | solution.py:22
  167.5 1.7 fusion.3
  179.9 2.7 collective-permute-start
  182.6 1.3 collective-permute-start.1
  185.0 8.5 %collective-permute-done.1 = bf16[1,352,128]{2,1,0:T(8,128)(2,1)S(1)} collective-permute-done((bf16[1,352,128]{2,1,0:T(8,128)(2,1)S(1)}, bf16[1,352,128]{2,1,0:T(8,128)(2,1)S(1)}, u32[]{:S(2)}, u32[]{:S(2)}) %collective-permute-start.1) | collective-permute-done | bytes 90144 | tf_op jit(solution)/shard_map/ppermute | solution.py:16
  194.1 2.4 fusion.34
  205.5 6.8 %add_convert_fusion = bf16[5632,512]{1,0:T(8,128)(2,1)} fusion(bf16[5632,512]{1,0:T(8,128)(2,1)} %bitcast.124, bf16[5632,128]{1,0:T(8,128)(2,1)S(1)} %fusion.2, bf16[512,128]{1,0:T(8,128)(2,1)S(1)} %copy-done), kind=kOutput, calls=%fused_computation.1 | convolution fusion | flops 746848256 | bytes 13107200 | tf_op jit(solution)/shard_map/dot_general | solution.py:92
  212.3 97.3 %all-reduce.5.cloned.1.call-done = (f32[3,3,128,128]{3,2,1,0:T(8,128)}, f32[128,512]{1,0:T(8,128)}) async-done(((f32[3,3,128,128]{3,2,1,0:T(8,128)}, f32[128,512]{1,0:T(8,128)}), (f32[3,3,128,128]{3,2,1,0:T(8,128)}, f32[128,512]{1,0:T(8,128)})) %all-reduce.5.cloned.1.call-update) | async-done | bytes 851984 | tf_op jit(solution)/shard_map/psum | solution.py:100
  309.6 1.7 broadcast_multiply_fusion.1
  311.3 1.9 broadcast_multiply_fusion
  313.2 55.1 %reduce-scatter.4.cloned.1.call-done = f32[32,128]{1,0:T(8,128)} async-done(((f32[512,128]{1,0:T(8,128)}), f32[32,128]{1,0:T(8,128)}) %reduce-scatter.4.cloned.1.call-update) | async-done | bytes 16400
  (78 shorter events, 23.3 us)
Async XLA Ops:
  7.2 198.3 %copy-start = (bf16[512,128]{1,0:T(8,128)(2,1)S(1)}, bf16[512,128]{1,0:T(8,128)(2,1)}, u32[]{:S(2)}) copy-start(bf16[512,128]{1,0:T(8,128)(2,1)} %param.13) | copy-start | bytes 393220
  16.8 7.6 %copy-start.2 = (bf16[16,352,128]{2,1,0:T(8,128)(2,1)S(1)}, bf16[16,352,128]{2,1,0:T(8,128)(2,1)}, u32[]{:S(2)}) copy-start(bf16[16,352,128]{2,1,0:T(8,128)(2,1)} %param.9) | copy-start | bytes 4325380
  16.8 121.8 %all-to-all-start = ((bf16[256,352,32]{1,2,0:T(8,128)(2,1)}), bf16[256,352,32]{1,2,0:T(8,128)(2,1)}, u32[]{:S(2)}, u32[]{:S(2)}) async-start(bf16[256,352,32]{1,2,0:T(8,128)(2,1)} %copy.21), calls=%async_computation | async-start | bytes 12582912 | tf_op jit(solution)/shard_map/all_to_all | solution.py:41
  24.4 285.2 %all-reduce.5.cloned.1.call-start = ((), (), s32[]{:S(2)}) async-start(), calls=%async_computation.3 | async-start | bytes 1703936 | tf_op jit(solution)/shard_map/psum | solution.py:100
  24.6 5.0 %copy-start.11 = (bf16[16,352,128]{2,1,0:T(8,128)(2,1)S(1)}, bf16[16,352,128]{2,1,0:T(8,128)(2,1)}, u32[]{:S(2)}) copy-start(bf16[16,352,128]{2,1,0:T(8,128)(2,1)} %param.10) | copy-start | bytes 4325380
  24.6 14.6 %collective-permute-start.2 = (bf16[1,352,128]{2,1,0:T(8,128)(2,1)S(1)}, bf16[1,352,128]{2,1,0:T(8,128)(2,1)S(1)}, u32[]{:S(2)}, u32[]{:S(2)}) collective-permute-start(bf16[1,352,128]{2,1,0:T(8,128)(2,1)S(1)} %get-tuple-element.32), channel_id=1, source_target_pairs={{0,1},{1,2},{2,3},{3,4},{4,5},{5,6},{6,7},{7,8},{8,9},{9,10},{10,1... | collective-permute-start | bytes 270344 | tf_op jit(solution)/shard_map/ppermute | solution.py:15
  27.0 12.2 %collective-permute-start.3 = (bf16[1,352,128]{2,1,0:T(8,128)(2,1)S(1)}, bf16[1,352,128]{2,1,0:T(8,128)(2,1)S(1)}, u32[]{:S(2)}, u32[]{:S(2)}) collective-permute-start(bf16[1,352,128]{2,1,0:T(8,128)(2,1)S(1)} %get-tuple-element.33), channel_id=1, source_target_pairs={{1,0},{2,1},{3,2},{4,3},{5,4},{6,5},{7,6},{8,7},{9,8},{10,9},{11,1... | collective-permute-start | bytes 270344 | tf_op jit(solution)/shard_map/ppermute | solution.py:16
  153.1 8.5 %copy-start.12 = (bf16[16,352,128]{2,1,0:T(8,128)(2,1)S(1)}, bf16[16,352,128]{2,1,0:T(8,128)(2,1)}, u32[]{:S(2)}) copy-start(bf16[16,352,128]{2,1,0:T(8,128)(2,1)} %param.10) | copy-start | bytes 4325380
  161.6 5.8 %copy-start.1 = (bf16[16,352,512]{2,1,0:T(8,128)(2,1)S(1)}, bf16[16,352,512]{2,1,0:T(8,128)(2,1)}, u32[]{:S(2)}) copy-start(bf16[16,352,512]{2,1,0:T(8,128)(2,1)} %copy.23) | copy-start | bytes 17301508
  161.6 5.8 %copy-start.14 = (pred[16,352,128]{2,1,0:T(32,128)(4,1)S(1)}, pred[16,352,128]{2,1,0:T(32,128)(4,1)}, u32[]{:S(2)}) copy-start(pred[16,352,128]{2,1,0:T(32,128)(4,1)} %broadcast_compare_fusion) | copy-start | bytes 2162692
  161.6 5.8 %copy-start.16 = (bf16[128,512]{1,0:T(8,128)(2,1)S(1)}, bf16[128,512]{1,0:T(8,128)(2,1)}, u32[]{:S(2)}) copy-start(bf16[128,512]{1,0:T(8,128)(2,1)} %param.15) | copy-start | bytes 393220
  167.5 1.7 copy-start.10
  169.2 1.4 copy-start.9
  170.5 1.4 copy-start.8
  171.9 1.4 copy-start.7
  173.3 1.4 copy-start.4
  175.2 1.4 copy-start.6
  176.6 1.4 copy-start.5
  179.9 5.2 %collective-permute-start = (bf16[1,352,128]{2,1,0:T(8,128)(2,1)S(1)}, bf16[1,352,128]{2,1,0:T(8,128)(2,1)S(1)}, u32[]{:S(2)}, u32[]{:S(2)}) collective-permute-start(bf16[1,352,128]{2,1,0:T(8,128)(2,1)S(1)} %get-tuple-element.36), channel_id=1, source_target_pairs={{0,1},{1,2},{2,3},{3,4},{4,5},{5,6},{6,7},{7,8},{8,9},{9,10},{10,1... | collective-permute-start | bytes 270344 | tf_op jit(solution)/shard_map/ppermute | solution.py:15
  182.6 11.0 %collective-permute-start.1 = (bf16[1,352,128]{2,1,0:T(8,128)(2,1)S(1)}, bf16[1,352,128]{2,1,0:T(8,128)(2,1)S(1)}, u32[]{:S(2)}, u32[]{:S(2)}) collective-permute-start(bf16[1,352,128]{2,1,0:T(8,128)(2,1)S(1)} %get-tuple-element.37), channel_id=1, source_target_pairs={{1,0},{2,1},{3,2},{4,3},{5,4},{6,5},{7,6},{8,7},{9,8},{10,9},{11,1... | collective-permute-start | bytes 270344 | tf_op jit(solution)/shard_map/ppermute | solution.py:16
  184.8 183.4 %reduce-scatter.4.cloned.1.call-start = ((), (), s32[]{:S(2)}) async-start(), calls=%async_computation.2 | async-start | bytes 278528
  194.1 2.4 copy-start.15
  200.5 2.4 slice-start
  201.6 2.0 slice-start.1
  (2 other events, 2.5 us)
Sparse Core Ops, SparseCore 0:
  184.9 124.6 all-reduce.4
  313.1 55.1 reduce-scatter.3
where the time goes:
time: 378 us; the launch traced here: 377 us
  waiting for transfers between devices  254 us (67%)
  local copies, waits for them, and re-layouts  48.8 us (13%)
  matrix products  25.6 us (7%)
  other arithmetic  18 us (5%)
  starting transfers between devices  15.5 us (4%)
  between operations  14.4 us (4%)
    psum x1, waiting for transfers between devices, shards(): middle_total = lax.psum(middle_part, 'rows')  97.3 us
    all_to_all x1, waiting for transfers between devices, shards(): lax.all_to_all(output_grad, 'rows', split_axis=0, concat_axis=2, tiled=True)  93.3 us
    unnamed x3, waiting for transfers between devices  55.1 us
    unnamed x43, local copies, waits for them, and re-layouts  27.6 us
    dot_general x11, matrix products, contract_rows(): lax.dot_general(left, right, (((0,), (0,)), ((), ())), preferred_element_...  12 us
    ppermute x2, waiting for transfers between devices, with_halo(): after = lax.ppermute(leading, axis, down)  8.54 us
    select_n x1, local copies, waits for them, and re-layouts, shards(): masked_out = jnp.where(output_pre > 0, spatial, jnp.zeros_like(spatial))  8.53 us
    select_n x1, other arithmetic, shards(): masked_out = jnp.where(output_pre > 0, spatial, jnp.zeros_like(spatial))  8.04 us
  transfers between devices with their start and end apart: 7, of which 4 were waited for; matrix products, arithmetic and copies ran while one was open for 10% of the time, Pallas kernels for 0%

commit v1 on v0

--- a/solution.py
+++ b/solution.py
@@ -97,7 +97,7 @@
         .astype(jnp.bfloat16)
         .reshape(tile_rows, map_cols, channels)
     )
-    middle_total = lax.psum(middle_part, "rows")
+    middle_total = jnp.sum(lax.all_gather(middle_part, "rows"), axis=0)
     return (input_grad, first_wgrad, middle_total * factor, last_total * factor)
 
 

time: 378 us -> 442 us (1.17)
  waiting for transfers between devices: 254 us -> 311 us
  matrix products: 25.6 us -> 32.3 us
    all_gather x0 -> x1, waiting for transfers between devices: none -> 81.8 us  [shards(): middle_total = jnp.sum(lax.all_gather(middle_part, 'rows'), axis=0)]
    psum x1, waiting for transfers between devices: 97.3 us -> 75.5 us  [shards(): last_total = lax.psum(last_part, 'rows')]
    ppermute x2, waiting for transfers between devices: 8.54 us -> 2.88 us  [with_halo(): after = lax.ppermute(leading, axis, down)]
    unnamed x43 -> x45, local copies, waits for them, and re-layouts: 27.6 us -> 24.8 us
    unnamed x3 -> x4, waiting for transfers between devices: 55.1 us -> 57.7 us
  transfers between devices with their start and end apart: 7 -> 8, of which waited for: 4 -> 5; matrix products, arithmetic and copies ran while one was open for 10% -> 12% of each run, Pallas kernels for 0% -> 0%
where the time goes in v1:
time: 442 us; the launch traced here: 441 us
  waiting for transfers between devices  311 us (70%)
  local copies, waits for them, and re-layouts  46.2 us (10%)
  matrix products  32.3 us (7%)
  other arithmetic  21.6 us (5%)
  starting transfers between devices  15.8 us (4%)
  between operations  14.1 us (3%)
    all_to_all x1, waiting for transfers between devices, shards(): lax.all_to_all(output_grad, 'rows', split_axis=0, concat_axis=2, tiled=True)  93 us
    all_gather x1, waiting for transfers between devices, shards(): middle_total = jnp.sum(lax.all_gather(middle_part, 'rows'), axis=0)  81.8 us
    psum x1, waiting for transfers between devices, shards(): last_total = lax.psum(last_part, 'rows')  75.5 us
    unnamed x4, waiting for transfers between devices  57.7 us
    unnamed x45, local copies, waits for them, and re-layouts  24.8 us
    dot_general x11, matrix products, contract_rows(): lax.dot_general(left, right, (((0,), (0,)), ((), ())), preferred_element_...  15.8 us
  transfers between devices with their start and end apart: 8, of which 5 were waited for; matrix products, arithmetic and copies ran while one was open for 12% of the time, Pallas kernels for 0%

profile of v1, /device:TPU:0, one launch (start us, length us, event | category | flops | bytes accessed | tf_op | source)
XLA Modules:
  0.0 441.0 jit_solution(7111158011106145655)
XLA Ops:
  7.2 9.7 %copy.21 = bf16[256,352,32]{1,2,0:T(8,128)(2,1)} copy(bf16[256,352,32]{0,2,1:T(8,128)(2,1)} %param.12) | data formatting | bytes 11534336 | tf_op args[4]
  16.9 7.6 %all-to-all-start = ((bf16[256,352,32]{1,2,0:T(8,128)(2,1)}), bf16[256,352,32]{1,2,0:T(8,128)(2,1)}, u32[]{:S(2)}, u32[]{:S(2)}) async-start(bf16[256,352,32]{1,2,0:T(8,128)(2,1)} %copy.21), calls=%async_computation | async-start | bytes 12582912 | tf_op jit(solution)/shard_map/all_to_all | solution.py:41
  24.6 2.4 collective-permute-start.2
  27.1 1.3 collective-permute-start.3
  30.9 8.3 %copy.20 = bf16[16,352,512]{1,2,0:T(8,128)(2,1)} copy(bf16[16,352,512]{2,1,0:T(8,128)(2,1)} %param.11) | data formatting | bytes 11534336 | tf_op args[3]
  39.2 1.9 pad_maximum_fusion.1
  41.6 4.0 fusion.33
  45.6 93.0 %all-to-all-done = bf16[256,352,32]{1,2,0:T(8,128)(2,1)} async-done(((bf16[256,352,32]{1,2,0:T(8,128)(2,1)}), bf16[256,352,32]{1,2,0:T(8,128)(2,1)}, u32[]{:S(2)}, u32[]{:S(2)}) %all-to-all-start) | async-done | bytes 5767200 | tf_op jit(solution)/shard_map/all_to_all | solution.py:41
  138.7 6.4 %copy.22 = bf16[16,352,16,32]{1,3,2,0:T(8,128)(2,1)} copy(bf16[16,352,16,32]{1,3,0,2:T(8,128)(2,1)} %bitcast.3) | data formatting | bytes 11534336 | tf_op jit(solution)/shard_map/all_to_all | solution.py:41
  145.1 8.1 %compare_select_fusion = bf16[16,352,512]{1,2,0:T(8,128)(2,1)} fusion(bf16[16,352,512]{1,2,0:T(8,128)(2,1)} %copy.20, bf16[16,352,16,32]{1,3,2,0:T(8,128)(2,1)} %copy.22), kind=kLoop, calls=%fused_computation | loop fusion | flops 5767168 | bytes 17301504 | tf_op jit(solution)/shard_map/jit(_where)/select_n | solution.py:42
  153.2 5.7 %fusion.8 = f32[128,512]{1,0:T(8,128)} fusion(bf16[16,352,512]{1,2,0:T(8,128)(2,1)} %compare_select_fusion, bf16[16,352,128]{2,1,0:T(8,128)(2,1)S(1)} %copy-done.10), kind=kOutput, calls=%fused_computation.28 | convolution fusion | flops 738918400 | bytes 7471104 | tf_op jit(solution)/shard_map/dot_general | solution.py:22
  158.9 8.5 %copy.23 = bf16[16,352,512]{2,1,0:T(8,128)(2,1)} copy(bf16[16,352,512]{1,2,0:T(8,128)(2,1)} %compare_select_fusion) | data formatting | bytes 11534336 | tf_op jit(solution)/shard_map/jit(_where)/select_n | solution.py:42
  167.5 4.6 %fusion.3 = bf16[5632,128]{1,0:T(8,128)(2,1)S(1)} fusion(pred[5632,128]{1,0:T(32,128)(4,1)} %bitcast.150, bf16[5632,512]{1,0:T(8,128)(2,1)} %bitcast.125, bf16[128,512]{1,0:T(8,128)(2,1)S(1)} %copy-done.17), kind=kOutput, calls=%fused_computation.13 | convolution fusion | flops 739639296 | bytes 8060928 | tf_op jit(solution)/shard_map/dot_general | solution.py:48
  175.2 2.7 collective-permute-start
  177.9 1.5 collective-permute-start.1
  186.1 2.9 collective-permute-done.1
  189.4 2.4 fusion.34
  201.2 2.0 convolution_bitcast_fusion.1
  204.1 6.8 %add_convert_fusion = bf16[5632,512]{1,0:T(8,128)(2,1)} fusion(bf16[5632,512]{1,0:T(8,128)(2,1)} %bitcast.126, bf16[5632,128]{1,0:T(8,128)(2,1)S(1)} %fusion.2, bf16[512,128]{1,0:T(8,128)(2,1)S(1)} %copy-done), kind=kOutput, calls=%fused_computation.1 | convolution fusion | flops 746848256 | bytes 13107200 | tf_op jit(solution)/shard_map/dot_general | solution.py:92
  211.0 75.5 %all-reduce.4.cloned.1.call-done = f32[128,512]{1,0:T(8,128)} async-done(((f32[128,512]{1,0:T(8,128)}), f32[128,512]{1,0:T(8,128)}) %all-reduce.4.cloned.1.call-update) | async-done | bytes 262160 | tf_op jit(solution)/shard_map/psum | solution.py:47
  286.5 1.7 broadcast_multiply_fusion.1
  288.2 57.7 %reduce-scatter.4.cloned.1.call-done = f32[32,128]{1,0:T(8,128)} async-done(((f32[512,128]{1,0:T(8,128)}), f32[32,128]{1,0:T(8,128)}) %reduce-scatter.4.cloned.1.call-update) | async-done | bytes 16400
  347.4 81.8 %all-gather.3.cloned.1.call-done = f32[48,3,128,128]{3,2,1,0:T(8,128)} async-done(((f32[3,3,128,128]{3,2,1,0:T(8,128)}), f32[48,3,128,128]{3,2,1,0:T(8,128)}) %all-gather.3.cloned.1.call-update) | async-done | bytes 9437200 | tf_op jit(solution)/shard_map/all_gather | solution.py:100
  429.2 4.4 reduce_sum.9
  (84 shorter events, 26.0 us)
Async XLA Ops:
  7.2 197.0 %copy-start = (bf16[512,128]{1,0:T(8,128)(2,1)S(1)}, bf16[512,128]{1,0:T(8,128)(2,1)}, u32[]{:S(2)}) copy-start(bf16[512,128]{1,0:T(8,128)(2,1)} %param.13) | copy-start | bytes 393220
  16.9 7.6 %copy-start.1 = (bf16[16,352,128]{2,1,0:T(8,128)(2,1)S(1)}, bf16[16,352,128]{2,1,0:T(8,128)(2,1)}, u32[]{:S(2)}) copy-start(bf16[16,352,128]{2,1,0:T(8,128)(2,1)} %param.9) | copy-start | bytes 4325380
  16.9 121.8 %all-to-all-start = ((bf16[256,352,32]{1,2,0:T(8,128)(2,1)}), bf16[256,352,32]{1,2,0:T(8,128)(2,1)}, u32[]{:S(2)}, u32[]{:S(2)}) async-start(bf16[256,352,32]{1,2,0:T(8,128)(2,1)} %copy.21), calls=%async_computation | async-start | bytes 12582912 | tf_op jit(solution)/shard_map/all_to_all | solution.py:41
  24.5 262.0 %all-reduce.4.cloned.1.call-start = ((), (), s32[]{:S(2)}) async-start(), calls=%async_computation.2 | async-start | bytes 524288 | tf_op jit(solution)/shard_map/psum | solution.py:47
  24.6 5.0 %copy-start.9 = (bf16[16,352,128]{2,1,0:T(8,128)(2,1)S(1)}, bf16[16,352,128]{2,1,0:T(8,128)(2,1)}, u32[]{:S(2)}) copy-start(bf16[16,352,128]{2,1,0:T(8,128)(2,1)} %param.10) | copy-start | bytes 4325380
  24.6 14.6 %collective-permute-start.2 = (bf16[1,352,128]{2,1,0:T(8,128)(2,1)S(1)}, bf16[1,352,128]{2,1,0:T(8,128)(2,1)S(1)}, u32[]{:S(2)}, u32[]{:S(2)}) collective-permute-start(bf16[1,352,128]{2,1,0:T(8,128)(2,1)S(1)} %get-tuple-element.30), channel_id=1, source_target_pairs={{0,1},{1,2},{2,3},{3,4},{4,5},{5,6},{6,7},{7,8},{8,9},{9,10},{10,1... | collective-permute-start | bytes 270344 | tf_op jit(solution)/shard_map/ppermute | solution.py:15
  27.1 12.2 %collective-permute-start.3 = (bf16[1,352,128]{2,1,0:T(8,128)(2,1)S(1)}, bf16[1,352,128]{2,1,0:T(8,128)(2,1)S(1)}, u32[]{:S(2)}, u32[]{:S(2)}) collective-permute-start(bf16[1,352,128]{2,1,0:T(8,128)(2,1)S(1)} %get-tuple-element.31), channel_id=1, source_target_pairs={{1,0},{2,1},{3,2},{4,3},{5,4},{6,5},{7,6},{8,7},{9,8},{10,9},{11,1... | collective-permute-start | bytes 270344 | tf_op jit(solution)/shard_map/ppermute | solution.py:16
  145.1 8.2 %copy-start.10 = (bf16[16,352,128]{2,1,0:T(8,128)(2,1)S(1)}, bf16[16,352,128]{2,1,0:T(8,128)(2,1)}, u32[]{:S(2)}) copy-start(bf16[16,352,128]{2,1,0:T(8,128)(2,1)} %param.10) | copy-start | bytes 4325380
  158.9 8.5 %copy-start.17 = (bf16[128,512]{1,0:T(8,128)(2,1)S(1)}, bf16[128,512]{1,0:T(8,128)(2,1)}, u32[]{:S(2)}) copy-start(bf16[128,512]{1,0:T(8,128)(2,1)} %param.15) | copy-start | bytes 393220
  167.4 178.5 %reduce-scatter.4.cloned.1.call-start = ((), (), s32[]{:S(2)}) async-start(), calls=%async_computation.4 | async-start | bytes 278528
  167.4 4.6 %copy-start.3 = (bf16[16,352,128]{2,1,0:T(8,128)(2,1)S(1)}, bf16[16,352,128]{2,1,0:T(8,128)(2,1)}, u32[]{:S(2)}) copy-start(bf16[16,352,128]{2,1,0:T(8,128)(2,1)} %get-tuple-element.29) | copy-start | bytes 4325380
  174.7 4.8 %copy-start.8 = (bf16[16,352,128]{2,1,0:T(8,128)(2,1)S(1)}, bf16[16,352,128]{2,1,0:T(8,128)(2,1)}, u32[]{:S(2)}) copy-start(bf16[16,352,128]{2,1,0:T(8,128)(2,1)} %get-tuple-element.16) | copy-start | bytes 4325380
  175.2 10.8 %collective-permute-start = (bf16[1,352,128]{2,1,0:T(8,128)(2,1)S(1)}, bf16[1,352,128]{2,1,0:T(8,128)(2,1)S(1)}, u32[]{:S(2)}, u32[]{:S(2)}) collective-permute-start(bf16[1,352,128]{2,1,0:T(8,128)(2,1)S(1)} %get-tuple-element.34), channel_id=1, source_target_pairs={{0,1},{1,2},{2,3},{3,4},{4,5},{5,6},{6,7},{7,8},{8,9},{9,10},{10,1... | collective-permute-start | bytes 270344 | tf_op jit(solution)/shard_map/ppermute | solution.py:15
  177.9 11.0 %collective-permute-start.1 = (bf16[1,352,128]{2,1,0:T(8,128)(2,1)S(1)}, bf16[1,352,128]{2,1,0:T(8,128)(2,1)S(1)}, u32[]{:S(2)}, u32[]{:S(2)}) collective-permute-start(bf16[1,352,128]{2,1,0:T(8,128)(2,1)S(1)} %get-tuple-element.35), channel_id=1, source_target_pairs={{1,0},{2,1},{3,2},{4,3},{5,4},{6,5},{7,6},{8,7},{9,8},{10,9},{11,1... | collective-permute-start | bytes 270344 | tf_op jit(solution)/shard_map/ppermute | solution.py:16
  179.4 1.4 copy-start.7
  180.8 1.4 copy-start.6
  189.4 2.4 copy-start.12
  195.9 2.4 slice-start
  197.0 2.0 slice-start.1
  200.8 228.4 %all-gather.3.cloned.1.call-start = ((), (), s32[]{:S(2)}) async-start(), calls=%async_computation.3 | async-start | bytes 10027008 | tf_op jit(solution)/shard_map/all_gather | solution.py:100
  201.1 2.0 copy-start.15
  201.1 2.0 copy-start.16
  201.1 2.1 copy-start.13
  201.1 2.1 copy-start.14
  (4 other events, 5.2 us)
Sparse Core Ops, SparseCore 0:
  167.5 118.9 all-reduce.3
  290.0 55.8 reduce-scatter.3
  348.7 80.4 all-gather.2
